TPU v7x, 512 devices: a whole 4x8x8 slice. The times are simulated.
512 devices in a mesh: cls: 128 (over y, z, core), dp: 4 (over x).
Axes of the slice: x: 4, y: 8, z: 8, core: 2. Of those that a mesh axis runs over, the one named last changes fastest.
Arguments:
- images: bfloat16 [65536, 4096], P(('cls', 'dp')), may hold values from -6 to 6
- defocus: bfloat16 [65536], P(('cls', 'dp')), may hold values from 0.5 to 2
- classes: int32 [65536, 1], P(('cls', 'dp')), may hold values from 0 to 127; in each aligned block of 128 rows (0 to 127, 128 to 255, ...) at most 2 rows name the same one
- rotations: int32 [65536], P(('cls', 'dp')), may hold values from 0 to 63
- references: bfloat16 [128, 64, 4096], P('cls'), may hold values from -6 to 6
Outputs:
- refined: bfloat16 [128, 64, 4096], P('cls', 'dp')
- misfit: float32 [65536], P(('cls', 'dp'))
Inputs may be any that keep to these rules, and one draw needn't show every extreme that they name: `classes`: among the rows of one device no class is named by more than 2 particles, and in every draw some device has exactly 2 particles of one class.
All inputs are finite; a program needn't handle non-finite values.
Results may differ from a plain program's by a relative error of at most 0.008.
Values may be sent and summed in bfloat16 or wider, within the bound.
No kernel may reach another device: no remote copies, remote signals or barrier semaphores. Data moves between devices by JAX's collectives and lax.ppermute only.
A program may use at most 64 MiB of HBM per device.

v0:
```python
import jax
import jax.numpy as jnp
from jax import lax
from jax.sharding import PartitionSpec as P

SIDE = 64


def wave_table(side_count):
    pixel_index = jnp.arange(side_count * side_count, dtype=jnp.int32)
    half_side = side_count // 2
    row_freq = (pixel_index // side_count + half_side) % side_count - half_side
    col_freq = (pixel_index % side_count + half_side) % side_count - half_side
    return (row_freq * row_freq + col_freq * col_freq).astype(jnp.float32) / float(
        half_side * half_side
    )


def contrast(defocus_rows, radius):
    phase = 20.0 * defocus_rows.astype(jnp.float32)[:, None] * radius[None, :] + 0.1
    return -jnp.sin(phase) * jnp.exp(-0.5 * radius)[None, :]


def sweep_rows(table, image_rows, rotation_rows, defocus_rows, radius):
    row_total = image_rows.shape[0]
    block_rows = min(64, row_total)
    block_count = row_total // block_rows
    rotation_count = table.shape[0]
    labels = jnp.arange(rotation_count, dtype=jnp.int32)

    def advance(gradient, block_index):
        row_start = block_index * block_rows
        image_block = lax.dynamic_slice_in_dim(image_rows, row_start, block_rows, 0)
        rotation_block = lax.dynamic_slice_in_dim(rotation_rows, row_start, block_rows, 0)
        defocus_block = lax.dynamic_slice_in_dim(defocus_rows, row_start, block_rows, 0)
        selector = (rotation_block[:, None] == labels[None, :]).astype(jnp.bfloat16)
        tiles = jnp.dot(selector, table, preferred_element_type=jnp.float32)
        contrast_rows = contrast(defocus_block, radius)
        residual = contrast_rows * tiles - image_block.astype(jnp.float32)
        misfit_rows = jnp.mean(residual * residual, axis=1)
        weighted = (contrast_rows * residual).astype(jnp.bfloat16)
        gradient = gradient + lax.dot_general(
            selector, weighted, (((0,), (0,)), ((), ())), preferred_element_type=jnp.float32
        )
        return (gradient, misfit_rows)

    start_grad = jnp.zeros((rotation_count, image_rows.shape[1]), jnp.float32)
    gradient, misfit_blocks = lax.scan(
        advance, start_grad, jnp.arange(block_count, dtype=jnp.int32)
    )
    return (gradient, misfit_blocks.reshape(row_total))


def build_slots(
    images, defocus, rotations, class_rows, class_rank, rank_first, slot_width, count_cls
):
    particle_ids = jnp.arange(images.shape[0], dtype=jnp.int32)
    inside = (class_rank >= rank_first) & (class_rank < rank_first + slot_width)
    slot_of = jnp.where(inside, class_rows * slot_width + class_rank - rank_first, -1)
    slot_ids = jnp.arange(count_cls * slot_width, dtype=jnp.int32)
    slot_match = slot_ids[:, None] == slot_of[None, :]
    slot_live = jnp.any(slot_match, axis=1)
    slot_source = jnp.sum(jnp.where(slot_match, particle_ids[None, :], 0), axis=1)
    send_images = jnp.where(
        slot_live[:, None], jnp.take(images, slot_source, axis=0), jnp.zeros((), jnp.bfloat16)
    )
    send_rotation = jnp.where(slot_live, jnp.take(rotations, slot_source), -1)
    send_defocus = jnp.where(
        slot_live, jnp.take(defocus, slot_source).astype(jnp.float32), 0.0
    ).astype(jnp.bfloat16)
    return (send_images, send_rotation, send_defocus)


def shards(images, defocus, classes, rotations, references):
    count_cls = lax.axis_size("cls")
    count_dp = lax.axis_size("dp")
    particle_count = images.shape[0]
    pixel_count = images.shape[1]
    rotation_count = references.shape[1]
    capacity = max(2, 2 * particle_count // count_cls)
    slot_count = count_cls * capacity
    radius = wave_table(SIDE)
    class_rows = classes[:, 0]
    particle_ids = jnp.arange(particle_count, dtype=jnp.int32)
    earlier_same = (class_rows[:, None] == class_rows[None, :]) & (
        particle_ids[None, :] < particle_ids[:, None]
    )
    class_rank = jnp.sum(earlier_same.astype(jnp.int32), axis=1)
    slot_of = class_rows * capacity + class_rank
    slot_ids = jnp.arange(slot_count, dtype=jnp.int32)
    slot_match = slot_ids[:, None] == slot_of[None, :]
    send_images, send_rotation, send_defocus = build_slots(
        images, defocus, rotations, class_rows, class_rank, 0, capacity, count_cls
    )
    recv_images, recv_rotation, recv_defocus = (
        lax.all_to_all(
            send_images.reshape(count_cls, capacity, pixel_count),
            "cls",
            split_axis=0,
            concat_axis=0,
            tiled=True,
        ),
        lax.all_to_all(
            send_rotation.astype(jnp.bfloat16).reshape(count_cls, capacity),
            "cls",
            split_axis=0,
            concat_axis=0,
            tiled=True,
        ),
        lax.all_to_all(
            send_defocus.reshape(count_cls, capacity),
            "cls",
            split_axis=0,
            concat_axis=0,
            tiled=True,
        ),
    )
    image_slots = recv_images.reshape(slot_count, pixel_count)
    rotation_slots = recv_rotation.reshape(slot_count).astype(jnp.int32)
    defocus_slots = recv_defocus.reshape(slot_count)
    labels = jnp.arange(rotation_count, dtype=jnp.int32)
    local_counts = jnp.sum((rotation_slots[:, None] == labels[None, :]).astype(jnp.float32), axis=0)
    counts = lax.psum(local_counts, "dp")
    damping = 0.5 * counts + 1.0
    table = references[0]
    grad_first, unused_first = sweep_rows(table, image_slots, rotation_slots, defocus_slots, radius)
    share_rows = rotation_count // count_dp
    share_start = lax.axis_index("dp") * share_rows
    damping_share = lax.dynamic_slice_in_dim(damping, share_start, share_rows, 0)
    grad_summed = lax.psum(grad_first.astype(jnp.bfloat16), "dp").astype(jnp.float32)
    table_next = (table.astype(jnp.float32) - grad_summed / damping[:, None]).astype(jnp.bfloat16)
    grad_second, misfit_slots = sweep_rows(
        table_next, image_slots, rotation_slots, defocus_slots, radius
    )
    second_share = lax.psum_scatter(
        grad_second.astype(jnp.bfloat16), "dp", scatter_dimension=0, tiled=True
    ).astype(jnp.float32)
    anchor_next = lax.dynamic_slice_in_dim(table_next, share_start, share_rows, 0).astype(
        jnp.float32
    )
    refined = (anchor_next - second_share / damping_share[:, None]).astype(jnp.bfloat16)
    returned = lax.all_to_all(
        misfit_slots.reshape(count_cls, capacity), "cls", split_axis=0, concat_axis=0, tiled=True
    )
    returned_slots = returned.reshape(slot_count)
    misfit = jnp.sum(jnp.where(slot_match, returned_slots[:, None], 0.0), axis=0)
    return (refined.reshape(1, share_rows, pixel_count), misfit)


def solution(mesh):
    in_specs = (
        P(("cls", "dp"), None),
        P(("cls", "dp")),
        P(("cls", "dp"), None),
        P(("cls", "dp")),
        P("cls", None, None),
    )
    out_specs = (P("cls", "dp", None), P(("cls", "dp")))
    return jax.shard_map(shards, mesh=mesh, in_specs=in_specs, out_specs=out_specs, check_vma=False)
```

profile of v0, /device:TPU:1, one launch (start us, length us, event | category | flops | bytes accessed | tf_op | source)
XLA Modules:
  0.0 286.1 jit_solution(12018576768820509236)
XLA Ops:
  12.4 18.4 %all-to-all-start = ((bf16[128,1,2]{2,1,0:T(2,128)(2,1)}), bf16[128,1,2]{2,1,0:T(2,128)(2,1)S(1)}, u32[]{:S(2)}, u32[]{:S(2)}) async-start(bf16[128,1,2]{2,1,0:T(2,128)(2,1)} %copy.18), calls=%async_computation | async-start | bytes 131072 | tf_op jit(solution)/shard_map/all_to_all | solution.py:103
  42.4 10.0 %all-to-all-start.1 = ((bf16[128,1,2]{2,1,0:T(2,128)(2,1)}), bf16[128,1,2]{2,1,0:T(2,128)(2,1)S(1)}, u32[]{:S(2)}, u32[]{:S(2)}) async-start(bf16[128,1,2]{2,1,0:T(2,128)(2,1)} %copy.21), calls=%async_computation.1 | async-start | bytes 131072 | tf_op jit(solution)/shard_map/all_to_all | solution.py:110
  52.4 5.4 %broadcast_select_fusion.1 = bf16[128,2,4096]{2,1,0:T(2,128)(2,1)} fusion(pred[128,2]{1,0:T(8,128)(4,1)S(1)} %broadcast_in_dim.108, bf16[128,2,4096]{2,1,0:T(2,128)(2,1)} %gather.23, pred[128,2]{1,0:T(8,128)(4,1)S(1)} %compare_and_fusion), kind=kLoop, calls=%fused_computation.103 | loop fusion | flops 2097152 | bytes 4194816 | tf_op jit(solution)/shard_map/jit(_where)/select_n | solution.py:64
  57.8 6.2 %all-to-all-done.1 = bf16[128,1,2]{2,1,0:T(2,128)(2,1)S(1)} async-done(((bf16[128,1,2]{2,1,0:T(2,128)(2,1)}), bf16[128,1,2]{2,1,0:T(2,128)(2,1)S(1)}, u32[]{:S(2)}, u32[]{:S(2)}) %all-to-all-start.1) | async-done | bytes 544 | tf_op jit(solution)/shard_map/all_to_all | solution.py:110
  64.0 8.0 %all-to-all-start.2 = ((bf16[128,2,4096]{2,1,0:T(2,128)(2,1)}), bf16[128,2,4096]{2,1,0:T(2,128)(2,1)}, u32[]{:S(2)}, u32[]{:S(2)}) async-start(bf16[128,2,4096]{2,1,0:T(2,128)(2,1)} %broadcast_select_fusion.1), calls=%async_computation.2 | async-start | bytes 4194304 | tf_op jit(solution)/shard_map/all_to_all | solution.py:96
  72.9 50.8 %all-to-all-done.2 = bf16[128,2,4096]{2,1,0:T(2,128)(2,1)} async-done(((bf16[128,2,4096]{2,1,0:T(2,128)(2,1)}), bf16[128,2,4096]{2,1,0:T(2,128)(2,1)}, u32[]{:S(2)}, u32[]{:S(2)}) %all-to-all-start.2) | async-done | bytes 2097184 | tf_op jit(solution)/shard_map/all_to_all | solution.py:96
  123.7 4.1 %reshape.220 = bf16[256,4096]{1,0:T(8,128)(2,1)} reshape(bf16[128,2,4096]{2,1,0:T(2,128)(2,1)} %all-to-all-done.2) | data formatting | bytes 4194304 | tf_op jit(solution)/shard_map/reshape | solution.py:118
  127.9 26.6 %while.26 = (s32[]{:T(128)}, f32[64,4096]{1,0:T(8,128)S(1)}, s32[4]{0:T(128)S(1)}, s32[256]{0:T(256)S(1)}, bf16[256]{0:T(256)(128)(2,1)S(1)}, /*index=5*/bf16[64...) while((s32[]{:T(128)}, f32[64,4096]{1,0:T(8,128)S(1)}, ...), condition=%wide.region_4.5_spmd.clone.clone, body=%wide.region_3.4_spmd.clone.clone.sunk | while | flops 70181000 | bytes 3213917 | solution.py:48
  129.3 5.2 %convolution_add_fusion.4 = f32[64,4096]{1,0:T(8,128)S(1)} fusion(bf16[64,4096]{1,0:T(8,128)(2,1)S(1)} %get-tuple-element.389, f32[64,4096]{1,0:T(8,128)S(1)} %get-tuple-element.372, bf16[256,4096]{1,0:T(8,128)(2,1)} %get-tuple-element.390, s32[]{:T(128)S(6)} %select_n.653, f32[4096]{0:T(1024)S(1)} %get-tuple-element.344, ...), kind=kOutput, calls=%fused_computation.7.clone.1 | convolution fusion | flops 70000640 | bytes 3180037 | tf_op jit(solution)/shard_map/while/body/eval_jaxpr/dot_general | solution.py:42
  135.9 5.2 %convolution_add_fusion.4 = f32[64,4096]{1,0:T(8,128)S(1)} fusion(bf16[64,4096]{1,0:T(8,128)(2,1)S(1)} %get-tuple-element.389, f32[64,4096]{1,0:T(8,128)S(1)} %get-tuple-element.372, bf16[256,4096]{1,0:T(8,128)(2,1)} %get-tuple-element.390, s32[]{:T(128)S(6)} %select_n.653, f32[4096]{0:T(1024)S(1)} %get-tuple-element.344, ...), kind=kOutput, calls=%fused_computation.7.clone.1 | convolution fusion | flops 70000640 | bytes 3180037 | tf_op jit(solution)/shard_map/while/body/eval_jaxpr/dot_general | solution.py:42
  142.6 5.2 %convolution_add_fusion.4 = f32[64,4096]{1,0:T(8,128)S(1)} fusion(bf16[64,4096]{1,0:T(8,128)(2,1)S(1)} %get-tuple-element.389, f32[64,4096]{1,0:T(8,128)S(1)} %get-tuple-element.372, bf16[256,4096]{1,0:T(8,128)(2,1)} %get-tuple-element.390, s32[]{:T(128)S(6)} %select_n.653, f32[4096]{0:T(1024)S(1)} %get-tuple-element.344, ...), kind=kOutput, calls=%fused_computation.7.clone.1 | convolution fusion | flops 70000640 | bytes 3180037 | tf_op jit(solution)/shard_map/while/body/eval_jaxpr/dot_general | solution.py:42
  149.3 5.2 %convolution_add_fusion.4 = f32[64,4096]{1,0:T(8,128)S(1)} fusion(bf16[64,4096]{1,0:T(8,128)(2,1)S(1)} %get-tuple-element.389, f32[64,4096]{1,0:T(8,128)S(1)} %get-tuple-element.372, bf16[256,4096]{1,0:T(8,128)(2,1)} %get-tuple-element.390, s32[]{:T(128)S(6)} %select_n.653, f32[4096]{0:T(1024)S(1)} %get-tuple-element.344, ...), kind=kOutput, calls=%fused_computation.7.clone.1 | convolution fusion | flops 70000640 | bytes 3180037 | tf_op jit(solution)/shard_map/while/body/eval_jaxpr/dot_general | solution.py:42
  155.6 8.5 %psum.15 = f32[64]{0:T(128)S(1)} all-reduce(f32[64]{0:T(128)S(1)} %convert_reduce_fusion.1), channel_id=1, replica_groups=mesh['cls'=128,'dp'=4] {'dp'}, use_global_device_ids=true, to_apply=%region_7.8 | all-reduce | flops 64 | bytes 512 | tf_op jit(solution)/shard_map/psum | solution.py:123
  164.0 37.8 %all-reduce.2.cloned.1.call-done = bf16[64,4096]{1,0:T(8,128)(2,1)} async-done(((bf16[64,4096]{1,0:T(8,128)(2,1)}), bf16[64,4096]{1,0:T(8,128)(2,1)}) %all-reduce.2.cloned.1.call-update) | async-done | bytes 524304 | tf_op jit(solution)/shard_map/psum | solution.py:130
  203.9 41.9 %while.27 = (s32[]{:T(128)}, f32[64,4096]{1,0:T(8,128)S(1)}, f32[4,64]{1,0:T(4,128)S(1)}, s32[4]{0:T(128)S(1)}, s32[256]{0:T(256)S(1)}, /*index=5*/bf16[256]{0:T...) while((s32[]{:T(128)}, f32[64,4096]{1,0:T(8,128)S(1)}, ...), condition=%wide.region_10.11_spmd.clone.clone, body=%wide.region_8.10_spmd.clone.clone.sunk | while | flops 71753864 | bytes 5344617 | solution.py:48
  205.4 5.1 %multiply_reduce_fusion.2 = (f32[64]{0:T(128)S(1)}, f32[64,4096]{1,0:T(8,128)S(1)}) fusion(bf16[256,4096]{1,0:T(8,128)(2,1)} %get-tuple-element.432, s32[]{:T(128)S(6)} %select_n.658, bf16[64,4096]{1,0:T(8,128)(2,1)} %get-tuple-element.431, s32[64]{0:T(128)S(1)} %dynamic_slice.72, f32[4096]{0:T(1024)S(1)} %get-tuple-element.354, ...), kind=kOutput, calls=%fused_computation.60.clone.1 | convolution fusion | flops 35917760 | bytes 2130692 | tf_op jit(solution)/shard_map/while/body/eval_jaxpr/dot_general | solution.py:37
  210.5 3.9 %convolution_add_fusion.5 = f32[64,4096]{1,0:T(8,128)S(1)} fusion(f32[64,4096]{1,0:T(8,128)S(1)} %get-tuple-element.412, f32[64,4096]{1,0:T(8,128)S(1)} %get-tuple-element.356, f32[4096]{0:T(1024)S(1)} %get-tuple-element.354, f32[4096]{0:T(1024)S(1)} %get-tuple-element.355, f32[64]{0:T(128)S(1)} %convert_multiply_fusion.5, pred[]{:T(512)S(6)} %compare.12, ...), kind=kOutput, calls=%fused_computation.57.clone.1 | convolution fusion | flops 35655680 | bytes 3179009 | tf_op jit(solution)/shard_map/while/body/eval_jaxpr/dot_general | solution.py:42
  215.8 5.1 %multiply_reduce_fusion.2 = (f32[64]{0:T(128)S(1)}, f32[64,4096]{1,0:T(8,128)S(1)}) fusion(bf16[256,4096]{1,0:T(8,128)(2,1)} %get-tuple-element.432, s32[]{:T(128)S(6)} %select_n.658, bf16[64,4096]{1,0:T(8,128)(2,1)} %get-tuple-element.431, s32[64]{0:T(128)S(1)} %dynamic_slice.72, f32[4096]{0:T(1024)S(1)} %get-tuple-element.354, ...), kind=kOutput, calls=%fused_computation.60.clone.1 | convolution fusion | flops 35917760 | bytes 2130692 | tf_op jit(solution)/shard_map/while/body/eval_jaxpr/dot_general | solution.py:37
  220.9 3.9 %convolution_add_fusion.5 = f32[64,4096]{1,0:T(8,128)S(1)} fusion(f32[64,4096]{1,0:T(8,128)S(1)} %get-tuple-element.412, f32[64,4096]{1,0:T(8,128)S(1)} %get-tuple-element.356, f32[4096]{0:T(1024)S(1)} %get-tuple-element.354, f32[4096]{0:T(1024)S(1)} %get-tuple-element.355, f32[64]{0:T(128)S(1)} %convert_multiply_fusion.5, pred[]{:T(512)S(6)} %compare.12, ...), kind=kOutput, calls=%fused_computation.57.clone.1 | convolution fusion | flops 35655680 | bytes 3179009 | tf_op jit(solution)/shard_map/while/body/eval_jaxpr/dot_general | solution.py:42
  226.3 5.1 %multiply_reduce_fusion.2 = (f32[64]{0:T(128)S(1)}, f32[64,4096]{1,0:T(8,128)S(1)}) fusion(bf16[256,4096]{1,0:T(8,128)(2,1)} %get-tuple-element.432, s32[]{:T(128)S(6)} %select_n.658, bf16[64,4096]{1,0:T(8,128)(2,1)} %get-tuple-element.431, s32[64]{0:T(128)S(1)} %dynamic_slice.72, f32[4096]{0:T(1024)S(1)} %get-tuple-element.354, ...), kind=kOutput, calls=%fused_computation.60.clone.1 | convolution fusion | flops 35917760 | bytes 2130692 | tf_op jit(solution)/shard_map/while/body/eval_jaxpr/dot_general | solution.py:37
  236.8 5.1 %multiply_reduce_fusion.2 = (f32[64]{0:T(128)S(1)}, f32[64,4096]{1,0:T(8,128)S(1)}) fusion(bf16[256,4096]{1,0:T(8,128)(2,1)} %get-tuple-element.432, s32[]{:T(128)S(6)} %select_n.658, bf16[64,4096]{1,0:T(8,128)(2,1)} %get-tuple-element.431, s32[64]{0:T(128)S(1)} %dynamic_slice.72, f32[4096]{0:T(1024)S(1)} %get-tuple-element.354, ...), kind=kOutput, calls=%fused_computation.60.clone.1 | convolution fusion | flops 35917760 | bytes 2130692 | tf_op jit(solution)/shard_map/while/body/eval_jaxpr/dot_general | solution.py:37
  241.9 3.9 %convolution_add_fusion.5 = f32[64,4096]{1,0:T(8,128)S(1)} fusion(f32[64,4096]{1,0:T(8,128)S(1)} %get-tuple-element.412, f32[64,4096]{1,0:T(8,128)S(1)} %get-tuple-element.356, f32[4096]{0:T(1024)S(1)} %get-tuple-element.354, f32[4096]{0:T(1024)S(1)} %get-tuple-element.355, f32[64]{0:T(128)S(1)} %convert_multiply_fusion.5, pred[]{:T(512)S(6)} %compare.12, ...), kind=kOutput, calls=%fused_computation.57.clone.1 | convolution fusion | flops 35655680 | bytes 3179009 | tf_op jit(solution)/shard_map/while/body/eval_jaxpr/dot_general | solution.py:42
  247.4 16.5 %all-to-all-start.3 = ((f32[128,1,2]{2,1,0:T(1,128)}), f32[128,1,2]{2,1,0:T(1,128)S(1)}, u32[]{:S(2)}, u32[]{:S(2)}) async-start(f32[128,1,2]{2,1,0:T(1,128)} %bitcast.5), calls=%async_computation.4 | async-start | bytes 131072 | tf_op jit(solution)/shard_map/all_to_all | solution.py:142
  264.0 11.4 %all-to-all-done.3 = f32[128,1,2]{2,1,0:T(1,128)S(1)} async-done(((f32[128,1,2]{2,1,0:T(1,128)}), f32[128,1,2]{2,1,0:T(1,128)S(1)}, u32[]{:S(2)}, u32[]{:S(2)}) %all-to-all-start.3) | async-done | bytes 1056 | tf_op jit(solution)/shard_map/all_to_all | solution.py:142
  (97 shorter events, 36.3 us)
Async XLA Ops:
  7.2 27.0 %copy-start = (bf16[128,4096]{1,0:T(8,128)(2,1)S(1)}, bf16[128,4096]{1,0:T(8,128)(2,1)}, u32[]{:S(2)}) copy-start(bf16[128,4096]{1,0:T(8,128)(2,1)} %param.9) | copy-start | bytes 3145732
  12.4 29.9 %all-to-all-start = ((bf16[128,1,2]{2,1,0:T(2,128)(2,1)}), bf16[128,1,2]{2,1,0:T(2,128)(2,1)S(1)}, u32[]{:S(2)}, u32[]{:S(2)}) async-start(bf16[128,1,2]{2,1,0:T(2,128)(2,1)} %copy.18), calls=%async_computation | async-start | bytes 131072 | tf_op jit(solution)/shard_map/all_to_all | solution.py:103
  42.4 21.6 %all-to-all-start.1 = ((bf16[128,1,2]{2,1,0:T(2,128)(2,1)}), bf16[128,1,2]{2,1,0:T(2,128)(2,1)S(1)}, u32[]{:S(2)}, u32[]{:S(2)}) async-start(bf16[128,1,2]{2,1,0:T(2,128)(2,1)} %copy.21), calls=%async_computation.1 | async-start | bytes 131072 | tf_op jit(solution)/shard_map/all_to_all | solution.py:110
  64.0 59.8 %all-to-all-start.2 = ((bf16[128,2,4096]{2,1,0:T(2,128)(2,1)}), bf16[128,2,4096]{2,1,0:T(2,128)(2,1)}, u32[]{:S(2)}, u32[]{:S(2)}) async-start(bf16[128,2,4096]{2,1,0:T(2,128)(2,1)} %broadcast_select_fusion.1), calls=%async_computation.2 | async-start | bytes 4194304 | tf_op jit(solution)/shard_map/all_to_all | solution.py:96
  72.0 129.9 %all-reduce.2.cloned.1.call-start = ((), (), s32[]{:S(2)}) async-start(), calls=%async_computation.5 | async-start | bytes 1048576 | tf_op jit(solution)/shard_map/psum | solution.py:130
  72.9 55.0 %copy-start.1 = (bf16[1,64,4096]{2,1,0:T(8,128)(2,1)S(1)}, bf16[1,64,4096]{2,1,0:T(8,128)(2,1)}, u32[]{:S(2)}) copy-start(bf16[1,64,4096]{2,1,0:T(8,128)(2,1)} %param.13) | copy-start | bytes 1572868
  155.4 122.1 %reduce-scatter.2.cloned.1.call-start = ((), (), s32[]{:S(2)}) async-start(), calls=%async_computation.6 | async-start | bytes 655360 | tf_op jit(solution)/shard_map/reduce_scatter | solution.py:135
  247.4 28.0 %all-to-all-start.3 = ((f32[128,1,2]{2,1,0:T(1,128)}), f32[128,1,2]{2,1,0:T(1,128)S(1)}, u32[]{:S(2)}, u32[]{:S(2)}) async-start(f32[128,1,2]{2,1,0:T(1,128)} %bitcast.5), calls=%async_computation.4 | async-start | bytes 131072 | tf_op jit(solution)/shard_map/all_to_all | solution.py:142
Sparse Core Ops, SparseCore 0:
  155.5 46.3 all-reduce.1
  246.8 27.7 reduce-scatter.1
where the time goes:
time: 287 us; the launch traced here: 286 us
  waiting for transfers between devices  110 us (38%)
  matrix products  56.8 us (20%)
  starting transfers between devices  53.1 us (19%)
  local copies, waits for them, and re-layouts  22.4 us (8%)
  other arithmetic  15.5 us (5%)
  between operations  14.2 us (5%)
  blocking collectives  8.48 us (3%)
  loops' own time  5.48 us (2%)
    all_to_all x1, waiting for transfers between devices, shards(): lax.all_to_all(send_images.reshape(count_cls, capacity, pixel_count), 'cl...  50.8 us
    psum x1, waiting for transfers between devices, shards(): lax.psum(grad_first.astype(jnp.bfloat16), 'dp').astype(jnp.float32)  37.8 us
    dot_general x8, matrix products, advance(): lax.dot_general(selector, weighted, (((0,), (0,)), ((), ())), preferred_e...  36.5 us
    dot_general x4, matrix products, advance(): tiles = jnp.dot(selector, table, preferred_element_type=jnp.float32)  20.4 us
    all_to_all x1, starting transfers between devices, shards(): lax.all_to_all(send_rotation.astype(jnp.bfloat16).reshape(count_cls, capa...  18.4 us
    all_to_all x1, starting transfers between devices, shards(): lax.all_to_all(misfit_slots.reshape(count_cls, capacity), 'cls', split_ax...  16.5 us
    all_to_all x1, waiting for transfers between devices, shards(): lax.all_to_all(misfit_slots.reshape(count_cls, capacity), 'cls', split_ax...  11.4 us
    all_to_all x1, starting transfers between devices, shards(): lax.all_to_all(send_defocus.reshape(count_cls, capacity), 'cls', split_ax...  10 us
  transfers between devices with their start and end apart: 6, of which 5 were waited for; matrix products, arithmetic and copies ran while one was open for 6% of the time, Pallas kernels for 0%

commit v1 on v0

--- a/solution.py
+++ b/solution.py
@@ -127,7 +127,9 @@
     share_rows = rotation_count // count_dp
     share_start = lax.axis_index("dp") * share_rows
     damping_share = lax.dynamic_slice_in_dim(damping, share_start, share_rows, 0)
-    grad_summed = lax.psum(grad_first.astype(jnp.bfloat16), "dp").astype(jnp.float32)
+    grad_summed = jnp.sum(lax.all_gather(grad_first.astype(jnp.bfloat16), "dp"), axis=0).astype(
+        jnp.float32
+    )
     table_next = (table.astype(jnp.float32) - grad_summed / damping[:, None]).astype(jnp.bfloat16)
     grad_second, misfit_slots = sweep_rows(
         table_next, image_slots, rotation_slots, defocus_slots, radius

time: 287 us -> 270 us (0.941)
  waiting for transfers between devices: 110 us -> 94.4 us
    psum x1 -> x0, waiting for transfers between devices: 37.8 us -> none  [shards(): lax.psum(grad_first.astype(jnp.bfloat16), 'dp').astype(jnp.float32)]
    all_gather x0 -> x1, waiting for transfers between devices: none -> 22.2 us  [shards(): lax.all_gather(grad_first.astype(jnp.bfloat16), 'dp')]
where the time goes in v1:
time: 270 us; the launch traced here: 269 us
  waiting for transfers between devices  94.4 us (35%)
  matrix products  56.8 us (21%)
  starting transfers between devices  51.1 us (19%)
  local copies, waits for them, and re-layouts  22.4 us (8%)
  other arithmetic  16.4 us (6%)
  between operations  14.3 us (5%)
  blocking collectives  8.48 us (3%)
  loops' own time  5.48 us (2%)
    all_to_all x1, waiting for transfers between devices, shards(): lax.all_to_all(send_images.reshape(count_cls, capacity, pixel_count), 'cl...  50.8 us
    dot_general x8, matrix products, advance(): lax.dot_general(selector, weighted, (((0,), (0,)), ((), ())), preferred_e...  36.5 us
    all_gather x1, waiting for transfers between devices, shards(): lax.all_gather(grad_first.astype(jnp.bfloat16), 'dp')  22.2 us
    dot_general x4, matrix products, advance(): tiles = jnp.dot(selector, table, preferred_element_type=jnp.float32)  20.4 us
    all_to_all x1, starting transfers between devices, shards(): lax.all_to_all(send_rotation.astype(jnp.bfloat16).reshape(count_cls, capa...  18.4 us
    all_to_all x1, starting transfers between devices, shards(): lax.all_to_all(misfit_slots.reshape(count_cls, capacity), 'cls', split_ax...  14.5 us
    all_to_all x1, waiting for transfers between devices, shards(): lax.all_to_all(misfit_slots.reshape(count_cls, capacity), 'cls', split_ax...  11.4 us
    all_to_all x1, starting transfers between devices, shards(): lax.all_to_all(send_defocus.reshape(count_cls, capacity), 'cls', split_ax...  10 us
  transfers between devices with their start and end apart: 6, of which 5 were waited for; matrix products, arithmetic and copies ran while one was open for 6% of the time, Pallas kernels for 0%

profile of v1, /device:TPU:1, one launch (start us, length us, event | category | flops | bytes accessed | tf_op | source)
XLA Modules:
  0.0 269.4 jit_solution(612686409037477378)
XLA Ops:
  12.4 18.4 %all-to-all-start = ((bf16[128,1,2]{2,1,0:T(2,128)(2,1)}), bf16[128,1,2]{2,1,0:T(2,128)(2,1)S(1)}, u32[]{:S(2)}, u32[]{:S(2)}) async-start(bf16[128,1,2]{2,1,0:T(2,128)(2,1)} %copy.18), calls=%async_computation | async-start | bytes 131072 | tf_op jit(solution)/shard_map/all_to_all | solution.py:103
  42.4 10.0 %all-to-all-start.1 = ((bf16[128,1,2]{2,1,0:T(2,128)(2,1)}), bf16[128,1,2]{2,1,0:T(2,128)(2,1)S(1)}, u32[]{:S(2)}, u32[]{:S(2)}) async-start(bf16[128,1,2]{2,1,0:T(2,128)(2,1)} %copy.21), calls=%async_computation.1 | async-start | bytes 131072 | tf_op jit(solution)/shard_map/all_to_all | solution.py:110
  52.4 5.4 %broadcast_select_fusion.1 = bf16[128,2,4096]{2,1,0:T(2,128)(2,1)} fusion(pred[128,2]{1,0:T(8,128)(4,1)S(1)} %broadcast_in_dim.108, bf16[128,2,4096]{2,1,0:T(2,128)(2,1)} %gather.23, pred[128,2]{1,0:T(8,128)(4,1)S(1)} %compare_and_fusion), kind=kLoop, calls=%fused_computation.103 | loop fusion | flops 2097152 | bytes 4194816 | tf_op jit(solution)/shard_map/jit(_where)/select_n | solution.py:64
  57.8 6.2 %all-to-all-done.1 = bf16[128,1,2]{2,1,0:T(2,128)(2,1)S(1)} async-done(((bf16[128,1,2]{2,1,0:T(2,128)(2,1)}), bf16[128,1,2]{2,1,0:T(2,128)(2,1)S(1)}, u32[]{:S(2)}, u32[]{:S(2)}) %all-to-all-start.1) | async-done | bytes 544 | tf_op jit(solution)/shard_map/all_to_all | solution.py:110
  64.0 8.0 %all-to-all-start.2 = ((bf16[128,2,4096]{2,1,0:T(2,128)(2,1)}), bf16[128,2,4096]{2,1,0:T(2,128)(2,1)}, u32[]{:S(2)}, u32[]{:S(2)}) async-start(bf16[128,2,4096]{2,1,0:T(2,128)(2,1)} %broadcast_select_fusion.1), calls=%async_computation.2 | async-start | bytes 4194304 | tf_op jit(solution)/shard_map/all_to_all | solution.py:96
  72.9 50.8 %all-to-all-done.2 = bf16[128,2,4096]{2,1,0:T(2,128)(2,1)} async-done(((bf16[128,2,4096]{2,1,0:T(2,128)(2,1)}), bf16[128,2,4096]{2,1,0:T(2,128)(2,1)}, u32[]{:S(2)}, u32[]{:S(2)}) %all-to-all-start.2) | async-done | bytes 2097184 | tf_op jit(solution)/shard_map/all_to_all | solution.py:96
  123.7 4.1 %reshape.220 = bf16[256,4096]{1,0:T(8,128)(2,1)} reshape(bf16[128,2,4096]{2,1,0:T(2,128)(2,1)} %all-to-all-done.2) | data formatting | bytes 4194304 | tf_op jit(solution)/shard_map/reshape | solution.py:118
  127.9 26.7 %while.26 = (s32[]{:T(128)}, f32[64,4096]{1,0:T(8,128)S(1)}, s32[4]{0:T(128)S(1)}, s32[256]{0:T(256)S(1)}, bf16[256]{0:T(256)(128)(2,1)S(1)}, /*index=5*/bf16[64...) while((s32[]{:T(128)}, f32[64,4096]{1,0:T(8,128)S(1)}, ...), condition=%wide.region_4.5_spmd.clone.clone, body=%wide.region_3.4_spmd.clone.clone.sunk | while | flops 70181000 | bytes 3213917 | solution.py:48
  129.3 5.2 %convolution_add_fusion.4 = f32[64,4096]{1,0:T(8,128)S(1)} fusion(bf16[64,4096]{1,0:T(8,128)(2,1)S(1)} %get-tuple-element.389, f32[64,4096]{1,0:T(8,128)S(1)} %get-tuple-element.372, bf16[256,4096]{1,0:T(8,128)(2,1)} %get-tuple-element.390, s32[]{:T(128)S(6)} %select_n.653, f32[4096]{0:T(1024)S(1)} %get-tuple-element.344, ...), kind=kOutput, calls=%fused_computation.7.clone.1 | convolution fusion | flops 70000640 | bytes 3180037 | tf_op jit(solution)/shard_map/while/body/eval_jaxpr/dot_general | solution.py:42
  135.9 5.2 %convolution_add_fusion.4 = f32[64,4096]{1,0:T(8,128)S(1)} fusion(bf16[64,4096]{1,0:T(8,128)(2,1)S(1)} %get-tuple-element.389, f32[64,4096]{1,0:T(8,128)S(1)} %get-tuple-element.372, bf16[256,4096]{1,0:T(8,128)(2,1)} %get-tuple-element.390, s32[]{:T(128)S(6)} %select_n.653, f32[4096]{0:T(1024)S(1)} %get-tuple-element.344, ...), kind=kOutput, calls=%fused_computation.7.clone.1 | convolution fusion | flops 70000640 | bytes 3180037 | tf_op jit(solution)/shard_map/while/body/eval_jaxpr/dot_general | solution.py:42
  142.6 5.2 %convolution_add_fusion.4 = f32[64,4096]{1,0:T(8,128)S(1)} fusion(bf16[64,4096]{1,0:T(8,128)(2,1)S(1)} %get-tuple-element.389, f32[64,4096]{1,0:T(8,128)S(1)} %get-tuple-element.372, bf16[256,4096]{1,0:T(8,128)(2,1)} %get-tuple-element.390, s32[]{:T(128)S(6)} %select_n.653, f32[4096]{0:T(1024)S(1)} %get-tuple-element.344, ...), kind=kOutput, calls=%fused_computation.7.clone.1 | convolution fusion | flops 70000640 | bytes 3180037 | tf_op jit(solution)/shard_map/while/body/eval_jaxpr/dot_general | solution.py:42
  149.3 5.2 %convolution_add_fusion.4 = f32[64,4096]{1,0:T(8,128)S(1)} fusion(bf16[64,4096]{1,0:T(8,128)(2,1)S(1)} %get-tuple-element.389, f32[64,4096]{1,0:T(8,128)S(1)} %get-tuple-element.372, bf16[256,4096]{1,0:T(8,128)(2,1)} %get-tuple-element.390, s32[]{:T(128)S(6)} %select_n.653, f32[4096]{0:T(1024)S(1)} %get-tuple-element.344, ...), kind=kOutput, calls=%fused_computation.7.clone.1 | convolution fusion | flops 70000640 | bytes 3180037 | tf_op jit(solution)/shard_map/while/body/eval_jaxpr/dot_general | solution.py:42
  155.6 8.5 %psum.7 = f32[64]{0:T(128)S(1)} all-reduce(f32[64]{0:T(128)S(1)} %convert_reduce_fusion.1), channel_id=1, replica_groups=mesh['cls'=128,'dp'=4] {'dp'}, use_global_device_ids=true, to_apply=%region_7.8 | all-reduce | flops 64 | bytes 512 | tf_op jit(solution)/shard_map/psum | solution.py:123
  164.1 22.2 %all-gather.3.cloned.1.call-done = bf16[256,4096]{1,0:T(8,128)(2,1)} async-done(((bf16[64,4096]{1,0:T(8,128)(2,1)}), bf16[256,4096]{1,0:T(8,128)(2,1)}) %all-gather.3.cloned.1.call-update) | async-done | bytes 2097168 | tf_op jit(solution)/shard_map/all_gather | solution.py:130
  189.3 41.9 %while.27 = (s32[]{:T(128)}, f32[64,4096]{1,0:T(8,128)S(1)}, f32[4,64]{1,0:T(4,128)S(1)}, s32[4]{0:T(128)S(1)}, s32[256]{0:T(256)S(1)}, /*index=5*/bf16[256]{0:T...) while((s32[]{:T(128)}, f32[64,4096]{1,0:T(8,128)S(1)}, ...), condition=%wide.region_10.11_spmd.clone.clone, body=%wide.region_8.10_spmd.clone.clone.sunk | while | flops 71753864 | bytes 5344617 | solution.py:48
  190.7 5.1 %multiply_reduce_fusion.2 = (f32[64]{0:T(128)S(1)}, f32[64,4096]{1,0:T(8,128)S(1)}) fusion(bf16[256,4096]{1,0:T(8,128)(2,1)} %get-tuple-element.432, s32[]{:T(128)S(6)} %select_n.658, bf16[64,4096]{1,0:T(8,128)(2,1)} %get-tuple-element.431, s32[64]{0:T(128)S(1)} %dynamic_slice.72, f32[4096]{0:T(1024)S(1)} %get-tuple-element.354, ...), kind=kOutput, calls=%fused_computation.60.clone.1 | convolution fusion | flops 35917760 | bytes 2130692 | tf_op jit(solution)/shard_map/while/body/eval_jaxpr/dot_general | solution.py:37
  195.8 3.9 %convolution_add_fusion.5 = f32[64,4096]{1,0:T(8,128)S(1)} fusion(f32[64,4096]{1,0:T(8,128)S(1)} %get-tuple-element.412, f32[64,4096]{1,0:T(8,128)S(1)} %get-tuple-element.356, f32[4096]{0:T(1024)S(1)} %get-tuple-element.354, f32[4096]{0:T(1024)S(1)} %get-tuple-element.355, f32[64]{0:T(128)S(1)} %convert_multiply_fusion.5, pred[]{:T(512)S(6)} %compare.12, ...), kind=kOutput, calls=%fused_computation.57.clone.1 | convolution fusion | flops 35655680 | bytes 3179009 | tf_op jit(solution)/shard_map/while/body/eval_jaxpr/dot_general | solution.py:42
  201.2 5.1 %multiply_reduce_fusion.2 = (f32[64]{0:T(128)S(1)}, f32[64,4096]{1,0:T(8,128)S(1)}) fusion(bf16[256,4096]{1,0:T(8,128)(2,1)} %get-tuple-element.432, s32[]{:T(128)S(6)} %select_n.658, bf16[64,4096]{1,0:T(8,128)(2,1)} %get-tuple-element.431, s32[64]{0:T(128)S(1)} %dynamic_slice.72, f32[4096]{0:T(1024)S(1)} %get-tuple-element.354, ...), kind=kOutput, calls=%fused_computation.60.clone.1 | convolution fusion | flops 35917760 | bytes 2130692 | tf_op jit(solution)/shard_map/while/body/eval_jaxpr/dot_general | solution.py:37
  211.6 5.1 %multiply_reduce_fusion.2 = (f32[64]{0:T(128)S(1)}, f32[64,4096]{1,0:T(8,128)S(1)}) fusion(bf16[256,4096]{1,0:T(8,128)(2,1)} %get-tuple-element.432, s32[]{:T(128)S(6)} %select_n.658, bf16[64,4096]{1,0:T(8,128)(2,1)} %get-tuple-element.431, s32[64]{0:T(128)S(1)} %dynamic_slice.72, f32[4096]{0:T(1024)S(1)} %get-tuple-element.354, ...), kind=kOutput, calls=%fused_computation.60.clone.1 | convolution fusion | flops 35917760 | bytes 2130692 | tf_op jit(solution)/shard_map/while/body/eval_jaxpr/dot_general | solution.py:37
  216.7 3.9 %convolution_add_fusion.5 = f32[64,4096]{1,0:T(8,128)S(1)} fusion(f32[64,4096]{1,0:T(8,128)S(1)} %get-tuple-element.412, f32[64,4096]{1,0:T(8,128)S(1)} %get-tuple-element.356, f32[4096]{0:T(1024)S(1)} %get-tuple-element.354, f32[4096]{0:T(1024)S(1)} %get-tuple-element.355, f32[64]{0:T(128)S(1)} %convert_multiply_fusion.5, pred[]{:T(512)S(6)} %compare.12, ...), kind=kOutput, calls=%fused_computation.57.clone.1 | convolution fusion | flops 35655680 | bytes 3179009 | tf_op jit(solution)/shard_map/while/body/eval_jaxpr/dot_general | solution.py:42
  222.1 5.1 %multiply_reduce_fusion.2 = (f32[64]{0:T(128)S(1)}, f32[64,4096]{1,0:T(8,128)S(1)}) fusion(bf16[256,4096]{1,0:T(8,128)(2,1)} %get-tuple-element.432, s32[]{:T(128)S(6)} %select_n.658, bf16[64,4096]{1,0:T(8,128)(2,1)} %get-tuple-element.431, s32[64]{0:T(128)S(1)} %dynamic_slice.72, f32[4096]{0:T(1024)S(1)} %get-tuple-element.354, ...), kind=kOutput, calls=%fused_computation.60.clone.1 | convolution fusion | flops 35917760 | bytes 2130692 | tf_op jit(solution)/shard_map/while/body/eval_jaxpr/dot_general | solution.py:37
  227.2 3.9 %convolution_add_fusion.5 = f32[64,4096]{1,0:T(8,128)S(1)} fusion(f32[64,4096]{1,0:T(8,128)S(1)} %get-tuple-element.412, f32[64,4096]{1,0:T(8,128)S(1)} %get-tuple-element.356, f32[4096]{0:T(1024)S(1)} %get-tuple-element.354, f32[4096]{0:T(1024)S(1)} %get-tuple-element.355, f32[64]{0:T(128)S(1)} %convert_multiply_fusion.5, pred[]{:T(512)S(6)} %compare.12, ...), kind=kOutput, calls=%fused_computation.57.clone.1 | convolution fusion | flops 35655680 | bytes 3179009 | tf_op jit(solution)/shard_map/while/body/eval_jaxpr/dot_general | solution.py:42
  232.7 14.5 %all-to-all-start.3 = ((f32[128,1,2]{2,1,0:T(1,128)}), f32[128,1,2]{2,1,0:T(1,128)S(1)}, u32[]{:S(2)}, u32[]{:S(2)}) async-start(f32[128,1,2]{2,1,0:T(1,128)} %bitcast.6), calls=%async_computation.4 | async-start | bytes 131072 | tf_op jit(solution)/shard_map/all_to_all | solution.py:144
  247.3 11.4 %all-to-all-done.3 = f32[128,1,2]{2,1,0:T(1,128)S(1)} async-done(((f32[128,1,2]{2,1,0:T(1,128)}), f32[128,1,2]{2,1,0:T(1,128)S(1)}, u32[]{:S(2)}, u32[]{:S(2)}) %all-to-all-start.3) | async-done | bytes 1056 | tf_op jit(solution)/shard_map/all_to_all | solution.py:144
  (98 shorter events, 37.2 us)
Async XLA Ops:
  7.2 27.0 %copy-start = (bf16[128,4096]{1,0:T(8,128)(2,1)S(1)}, bf16[128,4096]{1,0:T(8,128)(2,1)}, u32[]{:S(2)}) copy-start(bf16[128,4096]{1,0:T(8,128)(2,1)} %param.9) | copy-start | bytes 3145732
  12.4 29.9 %all-to-all-start = ((bf16[128,1,2]{2,1,0:T(2,128)(2,1)}), bf16[128,1,2]{2,1,0:T(2,128)(2,1)S(1)}, u32[]{:S(2)}, u32[]{:S(2)}) async-start(bf16[128,1,2]{2,1,0:T(2,128)(2,1)} %copy.18), calls=%async_computation | async-start | bytes 131072 | tf_op jit(solution)/shard_map/all_to_all | solution.py:103
  42.4 21.6 %all-to-all-start.1 = ((bf16[128,1,2]{2,1,0:T(2,128)(2,1)}), bf16[128,1,2]{2,1,0:T(2,128)(2,1)S(1)}, u32[]{:S(2)}, u32[]{:S(2)}) async-start(bf16[128,1,2]{2,1,0:T(2,128)(2,1)} %copy.21), calls=%async_computation.1 | async-start | bytes 131072 | tf_op jit(solution)/shard_map/all_to_all | solution.py:110
  64.0 59.8 %all-to-all-start.2 = ((bf16[128,2,4096]{2,1,0:T(2,128)(2,1)}), bf16[128,2,4096]{2,1,0:T(2,128)(2,1)}, u32[]{:S(2)}, u32[]{:S(2)}) async-start(bf16[128,2,4096]{2,1,0:T(2,128)(2,1)} %broadcast_select_fusion.1), calls=%async_computation.2 | async-start | bytes 4194304 | tf_op jit(solution)/shard_map/all_to_all | solution.py:96
  72.0 114.3 %all-gather.3.cloned.1.call-start = ((), (), s32[]{:S(2)}) async-start(), calls=%async_computation.6 | async-start | bytes 2621440 | tf_op jit(solution)/shard_map/all_gather | solution.py:130
  72.9 55.0 %copy-start.1 = (bf16[1,64,4096]{2,1,0:T(8,128)(2,1)S(1)}, bf16[1,64,4096]{2,1,0:T(8,128)(2,1)}, u32[]{:S(2)}) copy-start(bf16[1,64,4096]{2,1,0:T(8,128)(2,1)} %param.13) | copy-start | bytes 1572868
  155.4 105.4 %reduce-scatter.2.cloned.1.call-start = ((), (), s32[]{:S(2)}) async-start(), calls=%async_computation.5 | async-start | bytes 655360 | tf_op jit(solution)/shard_map/reduce_scatter | solution.py:137
  232.7 26.0 %all-to-all-start.3 = ((f32[128,1,2]{2,1,0:T(1,128)}), f32[128,1,2]{2,1,0:T(1,128)S(1)}, u32[]{:S(2)}, u32[]{:S(2)}) async-start(f32[128,1,2]{2,1,0:T(1,128)} %bitcast.6), calls=%async_computation.4 | async-start | bytes 131072 | tf_op jit(solution)/shard_map/all_to_all | solution.py:144
Sparse Core Ops, SparseCore 0:
  155.5 30.7 all-gather.2
  232.1 25.2 reduce-scatter.1
